TPU v7x, 32 devices: a whole 2x2x4 slice. The times are simulated.
32 devices in a mesh: member: 2 (over x), gx: 16 (over z, y, core).
Axes of the slice: x: 2, y: 2, z: 4, core: 2. Of those that a mesh axis runs over, the one named last changes fastest.
Arguments:
- electric: float32 [3, 64, 256, 128], P(None, 'gx'), may hold values from -6 to 6
- magnetic: float32 [3, 64, 256, 128], P(None, 'gx'), may hold values from -6 to 6
- material: int32 [128, 256, 128], P(('member', 'gx')), parts along dimension 0, may hold values from 0 to 3, as said below
- permittivity: float32 [4], replicated, may hold values from 1 to 4
- pole_frequency: float32 [2], replicated, may hold values from 0.3 to 1.2
- pole_damping: float32 [2], replicated, may hold values from 0.05 to 1
- pole_strength: float32 [2], replicated, may hold values from 0.3 to 2
- frequencies: float32 [8], replicated, may hold values from 0.2 to 2
- plane_depth: int32 [4], replicated, may hold values from 1 to 126
- mode_fields: float32 [4, 4, 64, 256], P(None, None, 'gx'), may hold values from -40 to 40
Outputs:
- electric_final: float32 [3, 128, 256, 128], P(None, ('member', 'gx')), parts along dimension 1
- magnetic_final: float32 [3, 128, 256, 128], P(None, ('member', 'gx')), parts along dimension 1
- monitors: float32 [2, 4, 8, 4, 128, 256], P(None, None, None, None, ('member', 'gx')), parts along dimension 4
- intersection: float32 [4, 4, 8], P('member'), parts along dimension 0
There are 2 independent parts, one for each index of `member`. A program takes and returns all parts, laid end to end along the dimension named above; an argument that names none is the same for every part. Nothing has to cross between parts.
Inputs may be any that keep to these rules, and one draw needn't show every extreme that they name: Each 16-layer thickness profile stacks layers along the first dimension, each of one material, with a lateral lattice of material 0 cells in some layers; materials 2 and above are dispersive.
All inputs are finite; a program needn't handle non-finite values.
Results may differ from a plain program's by a relative error of at most 0.0003.
Values sent between devices are 32-bit elements; how exact they have to be, the bound alone decides.
A program may use at most 64 MiB of HBM per device.

v0:
```python
import math
import jax
import jax.numpy as jnp
from jax import lax
from jax.sharding import PartitionSpec as P

STEPS = 6
DT = 0.5


def shifted(value, axis, steps):
    count = lax.axis_size(axis)
    first, last = (max(0, -steps), min(count, count - steps))
    return lax.ppermute(value, axis, [(source, source + steps) for source in range(first, last)])


def zero_rim(field, direction):
    return jnp.zeros_like(lax.slice_in_dim(field, 0, 1, axis=direction))


def diff_ahead(field, direction, beyond):
    remainder = lax.slice_in_dim(field, 1, field.shape[direction], axis=direction)
    return jnp.concatenate([remainder, beyond], axis=direction) - field


def diff_behind(field, direction, preceding):
    remainder = lax.slice_in_dim(field, 0, field.shape[direction] - 1, axis=direction)
    return field - jnp.concatenate([preceding, remainder], axis=direction)


def ahead_open(field, direction):
    return diff_ahead(field, direction, zero_rim(field, direction))


def behind_open(field, direction):
    return diff_behind(field, direction, zero_rim(field, direction))


def curl_e(e_field, upper):
    first = ahead_open(e_field[2], 1) - ahead_open(e_field[1], 2)
    second = ahead_open(e_field[0], 2) - diff_ahead(e_field[2], 0, upper[1])
    third = diff_ahead(e_field[1], 0, upper[0]) - ahead_open(e_field[0], 1)
    return jnp.stack([first, second, third])


def curl_h(h_field, lower):
    first = behind_open(h_field[2], 1) - behind_open(h_field[1], 2)
    second = behind_open(h_field[0], 2) - diff_behind(h_field[2], 0, lower[1])
    third = diff_behind(h_field[1], 0, lower[0]) - behind_open(h_field[0], 1)
    return jnp.stack([first, second, third])


def coefficients(material, permittivity, pole_frequency, pole_damping, pole_strength):
    eps_cell = jnp.zeros(material.shape, jnp.float32)
    for kind_index in range(permittivity.shape[0]):
        eps_cell = eps_cell + jnp.where(material == kind_index, permittivity[kind_index], 0.0)
    damping = jnp.zeros(material.shape, jnp.float32)
    square = jnp.zeros(material.shape, jnp.float32)
    driving = jnp.zeros(material.shape, jnp.float32)
    offset = permittivity.shape[0] - pole_frequency.shape[0]
    for pole_index in range(pole_frequency.shape[0]):
        chosen = material == pole_index + offset
        freq_sq = pole_frequency[pole_index] * pole_frequency[pole_index]
        damping = damping + jnp.where(chosen, pole_damping[pole_index], 0.0)
        square = square + jnp.where(chosen, freq_sq, 0.0)
        driving = driving + jnp.where(chosen, pole_strength[pole_index] * freq_sq, 0.0)
    divisor = 1.0 + 0.5 * DT * damping
    retain = (1.0 - 0.5 * DT * damping) / divisor
    pulling = DT * driving / divisor
    spring = DT * square / divisor
    step_e = DT / eps_cell
    return (retain, pulling, spring, step_e)


def record(monitors, e_field, h_field, select, frequencies, step):
    plane_e = jnp.einsum("cxyz,zm->cmxy", e_field[:2], select, precision=lax.Precision.HIGHEST)
    plane_h = jnp.einsum("cxyz,zm->cmxy", h_field[:2], select, precision=lax.Precision.HIGHEST)
    planes = jnp.concatenate([plane_e, plane_h], axis=0)
    phase_e = (step + 1.0) * DT * frequencies
    phase_h = (step + 0.5) * DT * frequencies
    cosines = jnp.stack([jnp.cos(phase_e), jnp.cos(phase_e), jnp.cos(phase_h), jnp.cos(phase_h)])
    sine_part = -jnp.stack([jnp.sin(phase_e), jnp.sin(phase_e), jnp.sin(phase_h), jnp.sin(phase_h)])
    rotation = jnp.stack([cosines, sine_part])
    return monitors + rotation[:, :, :, None, None, None] * planes[None, :, None, :, :, :]


def project(monitors, mode_fields, scale):
    pairing = jnp.stack([mode_fields[3], -mode_fields[2], -mode_fields[1], mode_fields[0]])
    return scale * jnp.einsum(
        "rcfmxy,cmxy->rmf", monitors, pairing, precision=lax.Precision.HIGHEST
    )


def pole_update(current, polarized, e_field, curl_field, retain, pulling, spring, step_e):
    current = retain * current + pulling * e_field - spring * polarized
    polarized = polarized + DT * current
    e_field = e_field + step_e * (curl_field - current)
    return (current, polarized, e_field)


def on_device(
    electric,
    magnetic,
    material,
    permittivity,
    pole_frequency,
    pole_damping,
    pole_strength,
    frequencies,
    plane_depth,
    mode_fields,
):
    retain, pulling, spring, step_e = coefficients(
        material, permittivity, pole_frequency, pole_damping, pole_strength
    )
    slab_cells = electric.shape[1]
    width_y = electric.shape[2]
    depth_z = electric.shape[3]
    select = (jnp.arange(depth_z)[:, None] == plane_depth[None, :]).astype(jnp.float32)
    current = jnp.zeros_like(electric)
    polarized = jnp.zeros_like(electric)
    monitors = jnp.zeros(
        (2, 4, frequencies.shape[0], plane_depth.shape[0], slab_cells, width_y), jnp.float32
    )
    for step in range(STEPS):
        upper = shifted(electric[1:3, :1], "gx", -1)
        magnetic = magnetic - DT * curl_e(electric, upper)
        lower = shifted(magnetic[1:3, -1:], "gx", 1)
        curl_field = curl_h(magnetic, lower)
        current, polarized, electric = pole_update(
            current, polarized, electric, curl_field, retain, pulling, spring, step_e
        )
        monitors = record(monitors, electric, magnetic, select, frequencies, step)
    scale = 1.0 / math.sqrt(4.0 * slab_cells * lax.axis_size("gx") * width_y)
    partial_value = project(monitors, mode_fields, scale)
    intersection = lax.psum(partial_value, "gx")
    return (electric, magnetic, monitors, intersection)


def solution(mesh):
    in_specs = (
        P(None, "gx", None, None),
        P(None, "gx", None, None),
        P(("member", "gx"), None, None),
        P(),
        P(),
        P(),
        P(),
        P(),
        P(),
        P(None, None, "gx", None),
    )
    out_specs = (
        P(None, ("member", "gx"), None, None),
        P(None, ("member", "gx"), None, None),
        P(None, None, None, None, ("member", "gx"), None),
        P("member", None, None),
    )
    return jax.shard_map(
        on_device, mesh=mesh, in_specs=in_specs, out_specs=out_specs, check_vma=False
    )
```

profile of v0, /device:TPU:0, one launch (start us, length us, event | category | flops | bytes accessed | tf_op | source)
XLA Modules:
  0.0 158.4 jit_solution(6075497116907819001)
XLA Ops:
  0.6 1.0 slice.656
  1.7 1.4 collective-permute-start
  3.1 1.5 slice_bitcast_fusion.35
  4.6 0.6 fusion.102
  7.8 0.6 fusion.103
  8.4 0.6 fusion.101
  9.0 0.7 fusion.100
  11.3 1.6 subtract_divide_fusion
  13.0 4.4 %broadcast_multiply_fusion.2 = (f32[4,256,128]{2,1,0:T(8,128)S(1)}, f32[4,256,128]{2,1,0:T(8,128)S(1)}, f32[4,256,128]{2,1,0:T(8,128)S(1)}, f32[4,256,128]{2,1,0:T(8,128)S(1)}, f32[4,256,128]{2,1,0:T(8,128)S(1)}) fusion(pred[4,256,128]{2,1,0:T(8,128)(4,1)S(1)} %get-tuple-element.10, f32[]{:T(128)} %bitcast.25, ...), kind=kLoop, calls=%fused_computation.218 | loop fusion | flops 3932160 | bytes 3407912 | tf_op jit(solution)/shard_map/mul | solution.py:95
  17.9 1.0 copy-done
  19.3 1.0 copy-done.1
  20.7 3.0 %collective-permute-start.1 = (f32[2,1,256,128]{3,2,1,0:T(8,128)S(1)}, f32[2,1,256,128]{3,2,1,0:T(8,128)S(1)}, u32[]{:S(2)}, u32[]{:S(2)}) collective-permute-start(f32[2,1,256,128]{3,2,1,0:T(8,128)S(1)} %slice.850), channel_id=1, source_target_pairs={{0,1},{1,2},{2,3},{3,4},{4,5},{5,6},{6,7},{7,8},{8,9},{9,10},{10,1... | collective-permute-start | bytes 786440 | tf_op jit(solution)/shard_map/ppermute | solution.py:14
  23.8 0.6 convolution_bitcast_fusion.10
  24.9 0.7 subtract_bitcast_fusion.10
  26.7 1.3 collective-permute-start.2
  28.6 5.8 %collective-permute-done.2 = f32[2,1,256,128]{3,2,1,0:T(8,128)S(1)} collective-permute-done((f32[2,1,256,128]{3,2,1,0:T(8,128)S(1)}, f32[2,1,256,128]{3,2,1,0:T(8,128)S(1)}, u32[]{:S(2)}, u32[]{:S(2)}) %collective-permute-start.2) | collective-permute-done | bytes 262176 | tf_op jit(solution)/shard_map/ppermute | solution.py:14
  35.2 7.4 %collective-permute-start.3 = (f32[2,1,256,128]{3,2,1,0:T(8,128)S(1)}, f32[2,1,256,128]{3,2,1,0:T(8,128)S(1)}, u32[]{:S(2)}, u32[]{:S(2)}) collective-permute-start(f32[2,1,256,128]{3,2,1,0:T(8,128)S(1)} %slice.874), channel_id=1, source_target_pairs={{0,1},{1,2},{2,3},{3,4},{4,5},{5,6},{6,7},{7,8},{8,9},{9,10},{10,1... | collective-permute-start | bytes 786440 | tf_op jit(solution)/shard_map/ppermute | solution.py:14
  43.8 0.7 subtract_bitcast_fusion.8
  44.5 0.8 fusion.5
  46.0 1.3 collective-permute-start.4
  47.9 3.2 %collective-permute-done.4 = f32[2,1,256,128]{3,2,1,0:T(8,128)S(1)} collective-permute-done((f32[2,1,256,128]{3,2,1,0:T(8,128)S(1)}, f32[2,1,256,128]{3,2,1,0:T(8,128)S(1)}, u32[]{:S(2)}, u32[]{:S(2)}) %collective-permute-start.4) | collective-permute-done | bytes 262176 | tf_op jit(solution)/shard_map/ppermute | solution.py:14
  52.1 7.6 %collective-permute-start.5 = (f32[2,1,256,128]{3,2,1,0:T(8,128)S(1)}, f32[2,1,256,128]{3,2,1,0:T(8,128)S(1)}, u32[]{:S(2)}, u32[]{:S(2)}) collective-permute-start(f32[2,1,256,128]{3,2,1,0:T(8,128)S(1)} %slice.898), channel_id=1, source_target_pairs={{0,1},{1,2},{2,3},{3,4},{4,5},{5,6},{6,7},{7,8},{8,9},{9,10},{10,1... | collective-permute-start | bytes 786440 | tf_op jit(solution)/shard_map/ppermute | solution.py:14
  60.7 0.7 subtract_bitcast_fusion.6
  61.4 1.3 fusion.8
  63.4 1.3 collective-permute-start.6
  65.3 3.2 %collective-permute-done.6 = f32[2,1,256,128]{3,2,1,0:T(8,128)S(1)} collective-permute-done((f32[2,1,256,128]{3,2,1,0:T(8,128)S(1)}, f32[2,1,256,128]{3,2,1,0:T(8,128)S(1)}, u32[]{:S(2)}, u32[]{:S(2)}) %collective-permute-start.6) | collective-permute-done | bytes 262176 | tf_op jit(solution)/shard_map/ppermute | solution.py:14
  68.7 0.6 fusion.9
  69.5 7.4 %collective-permute-start.7 = (f32[2,1,256,128]{3,2,1,0:T(8,128)S(1)}, f32[2,1,256,128]{3,2,1,0:T(8,128)S(1)}, u32[]{:S(2)}, u32[]{:S(2)}) collective-permute-start(f32[2,1,256,128]{3,2,1,0:T(8,128)S(1)} %slice.922), channel_id=1, source_target_pairs={{0,1},{1,2},{2,3},{3,4},{4,5},{5,6},{6,7},{7,8},{8,9},{9,10},{10,1... | collective-permute-start | bytes 786440 | tf_op jit(solution)/shard_map/ppermute | solution.py:14
  78.1 0.7 subtract_bitcast_fusion.4
  78.8 1.2 fusion.11
  80.7 1.3 collective-permute-start.8
  82.6 3.2 %collective-permute-done.8 = f32[2,1,256,128]{3,2,1,0:T(8,128)S(1)} collective-permute-done((f32[2,1,256,128]{3,2,1,0:T(8,128)S(1)}, f32[2,1,256,128]{3,2,1,0:T(8,128)S(1)}, u32[]{:S(2)}, u32[]{:S(2)}) %collective-permute-start.8) | collective-permute-done | bytes 262176 | tf_op jit(solution)/shard_map/ppermute | solution.py:14
  86.2 0.6 fusion.12
  87.0 7.9 %collective-permute-start.9 = (f32[2,1,256,128]{3,2,1,0:T(8,128)S(1)}, f32[2,1,256,128]{3,2,1,0:T(8,128)S(1)}, u32[]{:S(2)}, u32[]{:S(2)}) collective-permute-start(f32[2,1,256,128]{3,2,1,0:T(8,128)S(1)} %slice.946), channel_id=1, source_target_pairs={{0,1},{1,2},{2,3},{3,4},{4,5},{5,6},{6,7},{7,8},{8,9},{9,10},{10,1... | collective-permute-start | bytes 786440 | tf_op jit(solution)/shard_map/ppermute | solution.py:14
  94.9 0.6 convolution_bitcast_fusion.2
  96.1 0.7 subtract_bitcast_fusion.2
  96.8 1.0 fusion.14
  98.5 1.5 collective-permute-start.10
  100.6 3.0 %collective-permute-done.10 = f32[2,1,256,128]{3,2,1,0:T(8,128)S(1)} collective-permute-done((f32[2,1,256,128]{3,2,1,0:T(8,128)S(1)}, f32[2,1,256,128]{3,2,1,0:T(8,128)S(1)}, u32[]{:S(2)}, u32[]{:S(2)}) %collective-permute-start.10) | collective-permute-done | bytes 262176 | tf_op jit(solution)/shard_map/ppermute | solution.py:14
  103.9 0.8 fusion.15
  104.8 8.3 %collective-permute-start.11 = (f32[2,1,256,128]{3,2,1,0:T(8,128)S(1)}, f32[2,1,256,128]{3,2,1,0:T(8,128)S(1)}, u32[]{:S(2)}, u32[]{:S(2)}) collective-permute-start(f32[2,1,256,128]{3,2,1,0:T(8,128)S(1)} %slice.970), channel_id=1, source_target_pairs={{0,1},{1,2},{2,3},{3,4},{4,5},{5,6},{6,7},{7,8},{8,9},{9,10},{10,1... | collective-permute-start | bytes 786440 | tf_op jit(solution)/shard_map/ppermute | solution.py:14
  113.1 0.6 convolution_bitcast_fusion
  114.3 0.7 subtract_bitcast_fusion
  115.0 1.4 fusion.17
  116.4 0.6 convolution_bitcast_fusion.1
  117.0 1.1 multiply_add_fusion
  118.2 7.0 %fusion.32 = f32[4,1,2,8,1,1]{3,1,5,4,2,0:T(1,128)S(1)} fusion(f32[2,4,8,4,4,256]{5,4,3,2,1,0:T(4,128)S(1)} %multiply_add_fusion, f32[4,4,4,256,1,1]{3,2,1,0,4,5:T(4,128)S(1)} %maximum_bitcast_fusion), kind=kOutput, calls=%fused_computation.61 | convolution fusion | flops 3145728 | bytes 1114368 | tf_op jit(solution)/shard_map/rcfmxy,cmxy->rmf/dot_general | solution.py:89
  125.2 33.2 %psum.7 = f32[2,4,8]{2,1,0:T(4,128)} all-reduce(f32[2,4,8]{2,1,0:T(4,128)S(1)} %fusion.84), channel_id=1, replica_groups=mesh['member'=2,'gx'=16] {'gx'}, use_global_device_ids=true, to_apply=%region_0.1 | all-reduce | flops 64 | bytes 512 | tf_op jit(solution)/shard_map/psum | solution.py:136
  (147 shorter events, 16.3 us)
Async XLA Ops:
  1.6 3.0 %copy-start.9 = (f32[2]{0:T(128)S(1)}, f32[2]{0:T(128)}, u32[]{:S(2)}) copy-start(f32[2]{0:T(128)} %param.14) | copy-start | bytes 28
  1.6 6.2 %copy-start.10 = (f32[2]{0:T(128)S(1)}, f32[2]{0:T(128)}, u32[]{:S(2)}) copy-start(f32[2]{0:T(128)} %param.15) | copy-start | bytes 28
  1.6 6.7 %copy-start.11 = (f32[2]{0:T(128)S(1)}, f32[2]{0:T(128)}, u32[]{:S(2)}) copy-start(f32[2]{0:T(128)} %param.16) | copy-start | bytes 28
  1.6 7.3 %copy-start.8 = (f32[4]{0:T(128)S(1)}, f32[4]{0:T(128)}, u32[]{:S(2)}) copy-start(f32[4]{0:T(128)} %param.13) | copy-start | bytes 52
  1.7 8.0 %copy-start.12 = (f32[8]{0:T(128)S(1)}, f32[8]{0:T(128)}, u32[]{:S(2)}) copy-start(f32[8]{0:T(128)} %param.17) | copy-start | bytes 100
  1.7 8.2 %copy-start.7 = (f32[4,4,4,256]{3,2,1,0:T(4,128)S(1)}, f32[4,4,4,256]{3,2,1,0:T(4,128)}, u32[]{:S(2)}) copy-start(f32[4,4,4,256]{3,2,1,0:T(4,128)} %param.19) | copy-start | bytes 196612
  1.7 9.7 %copy-start.5 = (s32[4,256,128]{2,1,0:T(8,128)S(1)}, s32[4,256,128]{2,1,0:T(8,128)}, u32[]{:S(2)}) copy-start(s32[4,256,128]{2,1,0:T(8,128)} %param.12) | copy-start | bytes 1572868
  1.7 17.2 %collective-permute-start = (f32[2,1,256,128]{3,2,1,0:T(8,128)S(1)}, f32[2,1,256,128]{3,2,1,0:T(8,128)S(1)}, u32[]{:S(2)}, u32[]{:S(2)}) collective-permute-start(f32[2,1,256,128]{3,2,1,0:T(8,128)S(1)} %slice.656), channel_id=1, source_target_pairs={{1,0},{2,1},{3,2},{4,3},{5,4},{6,5},{7,6},{8,7},{9,8},{10,9},{11,1... | collective-permute-start | bytes 786440 | tf_op jit(solution)/shard_map/ppermute | solution.py:14
  17.4 1.4 copy-start
  18.9 1.4 copy-start.1
  20.6 3.2 %copy-start.6 = (s32[4]{0:T(128)S(1)}, s32[4]{0:T(128)}, u32[]{:S(2)}) copy-start(s32[4]{0:T(128)} %param.18) | copy-start | bytes 52
  20.7 4.2 %collective-permute-start.1 = (f32[2,1,256,128]{3,2,1,0:T(8,128)S(1)}, f32[2,1,256,128]{3,2,1,0:T(8,128)S(1)}, u32[]{:S(2)}, u32[]{:S(2)}) collective-permute-start(f32[2,1,256,128]{3,2,1,0:T(8,128)S(1)} %slice.850), channel_id=1, source_target_pairs={{0,1},{1,2},{2,3},{3,4},{4,5},{5,6},{6,7},{7,8},{8,9},{9,10},{10,1... | collective-permute-start | bytes 786440 | tf_op jit(solution)/shard_map/ppermute | solution.py:14
  26.7 7.7 %collective-permute-start.2 = (f32[2,1,256,128]{3,2,1,0:T(8,128)S(1)}, f32[2,1,256,128]{3,2,1,0:T(8,128)S(1)}, u32[]{:S(2)}, u32[]{:S(2)}) collective-permute-start(f32[2,1,256,128]{3,2,1,0:T(8,128)S(1)} %slice.863), channel_id=1, source_target_pairs={{1,0},{2,1},{3,2},{4,3},{5,4},{6,5},{7,6},{8,7},{9,8},{10,9},{11,1... | collective-permute-start | bytes 786440 | tf_op jit(solution)/shard_map/ppermute | solution.py:14
  35.2 8.6 %collective-permute-start.3 = (f32[2,1,256,128]{3,2,1,0:T(8,128)S(1)}, f32[2,1,256,128]{3,2,1,0:T(8,128)S(1)}, u32[]{:S(2)}, u32[]{:S(2)}) collective-permute-start(f32[2,1,256,128]{3,2,1,0:T(8,128)S(1)} %slice.874), channel_id=1, source_target_pairs={{0,1},{1,2},{2,3},{3,4},{4,5},{5,6},{6,7},{7,8},{8,9},{9,10},{10,1... | collective-permute-start | bytes 786440 | tf_op jit(solution)/shard_map/ppermute | solution.py:14
  46.0 5.1 %collective-permute-start.4 = (f32[2,1,256,128]{3,2,1,0:T(8,128)S(1)}, f32[2,1,256,128]{3,2,1,0:T(8,128)S(1)}, u32[]{:S(2)}, u32[]{:S(2)}) collective-permute-start(f32[2,1,256,128]{3,2,1,0:T(8,128)S(1)} %slice.887), channel_id=1, source_target_pairs={{1,0},{2,1},{3,2},{4,3},{5,4},{6,5},{7,6},{8,7},{9,8},{10,9},{11,1... | collective-permute-start | bytes 786440 | tf_op jit(solution)/shard_map/ppermute | solution.py:14
  52.1 8.6 %collective-permute-start.5 = (f32[2,1,256,128]{3,2,1,0:T(8,128)S(1)}, f32[2,1,256,128]{3,2,1,0:T(8,128)S(1)}, u32[]{:S(2)}, u32[]{:S(2)}) collective-permute-start(f32[2,1,256,128]{3,2,1,0:T(8,128)S(1)} %slice.898), channel_id=1, source_target_pairs={{0,1},{1,2},{2,3},{3,4},{4,5},{5,6},{6,7},{7,8},{8,9},{9,10},{10,1... | collective-permute-start | bytes 786440 | tf_op jit(solution)/shard_map/ppermute | solution.py:14
  63.4 5.1 %collective-permute-start.6 = (f32[2,1,256,128]{3,2,1,0:T(8,128)S(1)}, f32[2,1,256,128]{3,2,1,0:T(8,128)S(1)}, u32[]{:S(2)}, u32[]{:S(2)}) collective-permute-start(f32[2,1,256,128]{3,2,1,0:T(8,128)S(1)} %slice.911), channel_id=1, source_target_pairs={{1,0},{2,1},{3,2},{4,3},{5,4},{6,5},{7,6},{8,7},{9,8},{10,9},{11,1... | collective-permute-start | bytes 786440 | tf_op jit(solution)/shard_map/ppermute | solution.py:14
  69.5 8.6 %collective-permute-start.7 = (f32[2,1,256,128]{3,2,1,0:T(8,128)S(1)}, f32[2,1,256,128]{3,2,1,0:T(8,128)S(1)}, u32[]{:S(2)}, u32[]{:S(2)}) collective-permute-start(f32[2,1,256,128]{3,2,1,0:T(8,128)S(1)} %slice.922), channel_id=1, source_target_pairs={{0,1},{1,2},{2,3},{3,4},{4,5},{5,6},{6,7},{7,8},{8,9},{9,10},{10,1... | collective-permute-start | bytes 786440 | tf_op jit(solution)/shard_map/ppermute | solution.py:14
  80.7 5.1 %collective-permute-start.8 = (f32[2,1,256,128]{3,2,1,0:T(8,128)S(1)}, f32[2,1,256,128]{3,2,1,0:T(8,128)S(1)}, u32[]{:S(2)}, u32[]{:S(2)}) collective-permute-start(f32[2,1,256,128]{3,2,1,0:T(8,128)S(1)} %slice.935), channel_id=1, source_target_pairs={{1,0},{2,1},{3,2},{4,3},{5,4},{6,5},{7,6},{8,7},{9,8},{10,9},{11,1... | collective-permute-start | bytes 786440 | tf_op jit(solution)/shard_map/ppermute | solution.py:14
  87.0 9.1 %collective-permute-start.9 = (f32[2,1,256,128]{3,2,1,0:T(8,128)S(1)}, f32[2,1,256,128]{3,2,1,0:T(8,128)S(1)}, u32[]{:S(2)}, u32[]{:S(2)}) collective-permute-start(f32[2,1,256,128]{3,2,1,0:T(8,128)S(1)} %slice.946), channel_id=1, source_target_pairs={{0,1},{1,2},{2,3},{3,4},{4,5},{5,6},{6,7},{7,8},{8,9},{9,10},{10,1... | collective-permute-start | bytes 786440 | tf_op jit(solution)/shard_map/ppermute | solution.py:14
  98.5 5.1 %collective-permute-start.10 = (f32[2,1,256,128]{3,2,1,0:T(8,128)S(1)}, f32[2,1,256,128]{3,2,1,0:T(8,128)S(1)}, u32[]{:S(2)}, u32[]{:S(2)}) collective-permute-start(f32[2,1,256,128]{3,2,1,0:T(8,128)S(1)} %slice.959), channel_id=1, source_target_pairs={{1,0},{2,1},{3,2},{4,3},{5,4},{6,5},{7,6},{8,7},{9,8},{10,9},{11,1... | collective-permute-start | bytes 786440 | tf_op jit(solution)/shard_map/ppermute | solution.py:14
  104.7 9.6 %copy-start.2 = (f32[3,4,256,128]{3,2,1,0:T(8,128)}, f32[3,4,256,128]{3,2,1,0:T(8,128)S(1)}, u32[]{:S(2)}) copy-start(f32[3,4,256,128]{3,2,1,0:T(8,128)S(1)} %fusion.15) | copy-start | bytes 4718596
  104.8 9.5 %collective-permute-start.11 = (f32[2,1,256,128]{3,2,1,0:T(8,128)S(1)}, f32[2,1,256,128]{3,2,1,0:T(8,128)S(1)}, u32[]{:S(2)}, u32[]{:S(2)}) collective-permute-start(f32[2,1,256,128]{3,2,1,0:T(8,128)S(1)} %slice.970), channel_id=1, source_target_pairs={{0,1},{1,2},{2,3},{3,4},{4,5},{5,6},{6,7},{7,8},{8,9},{9,10},{10,1... | collective-permute-start | bytes 786440 | tf_op jit(solution)/shard_map/ppermute | solution.py:14
  116.4 8.8 %copy-start.3 = (f32[3,4,256,128]{3,2,1,0:T(8,128)}, f32[3,4,256,128]{3,2,1,0:T(8,128)S(1)}, u32[]{:S(2)}) copy-start(f32[3,4,256,128]{3,2,1,0:T(8,128)S(1)} %fusion.17) | copy-start | bytes 4718596
  118.2 40.2 %copy-start.4 = (f32[2,4,8,4,4,256]{5,4,3,2,1,0:T(4,128)}, f32[2,4,8,4,4,256]{5,4,3,2,1,0:T(4,128)S(1)}, u32[]{:S(2)}) copy-start(f32[2,4,8,4,4,256]{5,4,3,2,1,0:T(4,128)S(1)} %multiply_add_fusion) | copy-start | bytes 3145732
where the time goes:
time: 159 us; the launch traced here: 158 us
  starting transfers between devices  49.9 us (31%)
  blocking collectives  33.2 us (21%)
  other arithmetic  22.6 us (14%)
  waiting for transfers between devices  21 us (13%)
  matrix products  13.9 us (9%)
  local copies, waits for them, and re-layouts  12.2 us (8%)
  between operations  5.55 us (3%)
    ppermute x12, starting transfers between devices, shifted(): lax.ppermute(value, axis, [(source, source + steps) for source in range(f...  49.9 us
    psum x1, blocking collectives, on_device(): intersection = lax.psum(partial_value, 'gx')  33.2 us
    ppermute x12, waiting for transfers between devices, shifted(): lax.ppermute(value, axis, [(source, source + steps) for source in range(f...  21 us
    dot_general x1, matrix products, project(): jnp.einsum('rcfmxy,cmxy->rmf', monitors, pairing, precision=lax.Precision...  6.99 us
    add x6, other arithmetic, pole_update(): e_field = e_field + step_e * (curl_field - current)  5.96 us
    mul x1, other arithmetic, pole_update(): current = retain * current + pulling * e_field - spring * polarized  4.4 us
    another operation x6, other arithmetic, curl_h(): return jnp.stack([first, second, third])  4.26 us
    dot_general x6, matrix products, record(): jnp.einsum('cxyz,zm->cmxy', h_field[:2], select, precision=lax.Precision....  3.47 us
  transfers between devices with their start and end apart: 12, of which 11 were waited for; matrix products, arithmetic and copies ran while one was open for 11% of the time, Pallas kernels for 0%

commit v1 on v0

--- a/solution.py
+++ b/solution.py
@@ -6,6 +6,11 @@
 
 STEPS = 6
 DT = 0.5
+
+
+def _check_skins(unit, axis_id):
+    current_block = jax.lax.all_gather(unit, axis_id)
+    return jnp.sum(current_block, 0)
 
 
 def shifted(value, axis, steps):
@@ -133,7 +138,7 @@
         monitors = record(monitors, electric, magnetic, select, frequencies, step)
     scale = 1.0 / math.sqrt(4.0 * slab_cells * lax.axis_size("gx") * width_y)
     partial_value = project(monitors, mode_fields, scale)
-    intersection = lax.psum(partial_value, "gx")
+    intersection = _check_skins(partial_value, "gx")
     return (electric, magnetic, monitors, intersection)
 
 

time: 159 us -> 152 us (0.956)
  blocking collectives: 33.2 us -> 25.5 us
    psum x1 -> x0, blocking collectives: 33.2 us -> none  [on_device(): intersection = lax.psum(partial_value, 'gx')]
    all_gather x0 -> x1, blocking collectives: none -> 25.5 us  [_check_skins(): current_block = jax.lax.all_gather(unit, axis_id)]
where the time goes in v1:
time: 152 us; the launch traced here: 151 us
  starting transfers between devices  49.9 us (33%)
  blocking collectives  25.5 us (17%)
  other arithmetic  23.2 us (15%)
  waiting for transfers between devices  21 us (14%)
  matrix products  13.9 us (9%)
  local copies, waits for them, and re-layouts  12.2 us (8%)
  between operations  5.55 us (4%)
    ppermute x12, starting transfers between devices, shifted(): lax.ppermute(value, axis, [(source, source + steps) for source in range(f...  49.9 us
    all_gather x1, blocking collectives, _check_skins(): current_block = jax.lax.all_gather(unit, axis_id)  25.5 us
    ppermute x12, waiting for transfers between devices, shifted(): lax.ppermute(value, axis, [(source, source + steps) for source in range(f...  21 us
    dot_general x1, matrix products, project(): jnp.einsum('rcfmxy,cmxy->rmf', monitors, pairing, precision=lax.Precision...  6.99 us
    add x6, other arithmetic, pole_update(): e_field = e_field + step_e * (curl_field - current)  5.96 us
    mul x1, other arithmetic, pole_update(): current = retain * current + pulling * e_field - spring * polarized  4.4 us
    another operation x6, other arithmetic, curl_h(): return jnp.stack([first, second, third])  4.26 us
    dot_general x6, matrix products, record(): jnp.einsum('cxyz,zm->cmxy', h_field[:2], select, precision=lax.Precision....  3.47 us
  transfers between devices with their start and end apart: 12, of which 11 were waited for; matrix products, arithmetic and copies ran while one was open for 11% of the time, Pallas kernels for 0%

profile of v1, /device:TPU:0, one launch (start us, length us, event | category | flops | bytes accessed | tf_op | source)
XLA Modules:
  0.0 151.3 jit_solution(5656615637664879562)
XLA Ops:
  0.6 1.0 slice.656
  1.7 1.4 collective-permute-start
  3.1 1.5 slice_bitcast_fusion.35
  4.6 0.6 fusion.102
  7.8 0.6 fusion.103
  8.4 0.6 fusion.101
  9.0 0.7 fusion.100
  11.3 1.6 %subtract_divide_fusion = (f32[4,256,128]{2,1,0:T(8,128)S(1)}, pred[4,256,128]{2,1,0:T(8,128)(4,1)S(1)}, pred[4,256,128]{2,1,0:T(8,128)(4,1)S(1)}) fusion(f32[]{:T(128)} %bitcast.25, f32[]{:T(128)} %bitcast.24, s32[4,256,128]{2,1,0:T(8,128)S(1)} %copy-done.5), kind=kLoop, calls=%fused_computation.181 | loop fusion | flops 1179648 | bytes 1310728 | tf_op jit(solution)/shard_map/div | solution.py:73
  13.0 4.4 %broadcast_multiply_fusion.2 = (f32[4,256,128]{2,1,0:T(8,128)S(1)}, f32[4,256,128]{2,1,0:T(8,128)S(1)}, f32[4,256,128]{2,1,0:T(8,128)S(1)}, f32[4,256,128]{2,1,0:T(8,128)S(1)}, f32[4,256,128]{2,1,0:T(8,128)S(1)}) fusion(pred[4,256,128]{2,1,0:T(8,128)(4,1)S(1)} %get-tuple-element.10, f32[]{:T(128)} %bitcast.25, ...), kind=kLoop, calls=%fused_computation.218 | loop fusion | flops 3932160 | bytes 3407912 | tf_op jit(solution)/shard_map/mul | solution.py:100
  17.9 1.0 copy-done
  19.3 1.0 copy-done.1
  20.7 3.0 %collective-permute-start.1 = (f32[2,1,256,128]{3,2,1,0:T(8,128)S(1)}, f32[2,1,256,128]{3,2,1,0:T(8,128)S(1)}, u32[]{:S(2)}, u32[]{:S(2)}) collective-permute-start(f32[2,1,256,128]{3,2,1,0:T(8,128)S(1)} %slice.850), channel_id=1, source_target_pairs={{0,1},{1,2},{2,3},{3,4},{4,5},{5,6},{6,7},{7,8},{8,9},{9,10},{10,1... | collective-permute-start | bytes 786440 | tf_op jit(solution)/shard_map/ppermute | solution.py:19
  24.9 0.7 subtract_bitcast_fusion.10
  26.7 1.3 collective-permute-start.2
  28.6 5.8 %collective-permute-done.2 = f32[2,1,256,128]{3,2,1,0:T(8,128)S(1)} collective-permute-done((f32[2,1,256,128]{3,2,1,0:T(8,128)S(1)}, f32[2,1,256,128]{3,2,1,0:T(8,128)S(1)}, u32[]{:S(2)}, u32[]{:S(2)}) %collective-permute-start.2) | collective-permute-done | bytes 262176 | tf_op jit(solution)/shard_map/ppermute | solution.py:19
  35.2 7.4 %collective-permute-start.3 = (f32[2,1,256,128]{3,2,1,0:T(8,128)S(1)}, f32[2,1,256,128]{3,2,1,0:T(8,128)S(1)}, u32[]{:S(2)}, u32[]{:S(2)}) collective-permute-start(f32[2,1,256,128]{3,2,1,0:T(8,128)S(1)} %slice.874), channel_id=1, source_target_pairs={{0,1},{1,2},{2,3},{3,4},{4,5},{5,6},{6,7},{7,8},{8,9},{9,10},{10,1... | collective-permute-start | bytes 786440 | tf_op jit(solution)/shard_map/ppermute | solution.py:19
  43.8 0.7 subtract_bitcast_fusion.8
  44.5 0.8 fusion.5
  46.0 1.3 collective-permute-start.4
  47.9 3.2 %collective-permute-done.4 = f32[2,1,256,128]{3,2,1,0:T(8,128)S(1)} collective-permute-done((f32[2,1,256,128]{3,2,1,0:T(8,128)S(1)}, f32[2,1,256,128]{3,2,1,0:T(8,128)S(1)}, u32[]{:S(2)}, u32[]{:S(2)}) %collective-permute-start.4) | collective-permute-done | bytes 262176 | tf_op jit(solution)/shard_map/ppermute | solution.py:19
  52.1 7.6 %collective-permute-start.5 = (f32[2,1,256,128]{3,2,1,0:T(8,128)S(1)}, f32[2,1,256,128]{3,2,1,0:T(8,128)S(1)}, u32[]{:S(2)}, u32[]{:S(2)}) collective-permute-start(f32[2,1,256,128]{3,2,1,0:T(8,128)S(1)} %slice.898), channel_id=1, source_target_pairs={{0,1},{1,2},{2,3},{3,4},{4,5},{5,6},{6,7},{7,8},{8,9},{9,10},{10,1... | collective-permute-start | bytes 786440 | tf_op jit(solution)/shard_map/ppermute | solution.py:19
  60.7 0.7 subtract_bitcast_fusion.6
  61.4 1.3 fusion.8
  63.4 1.3 collective-permute-start.6
  65.3 3.2 %collective-permute-done.6 = f32[2,1,256,128]{3,2,1,0:T(8,128)S(1)} collective-permute-done((f32[2,1,256,128]{3,2,1,0:T(8,128)S(1)}, f32[2,1,256,128]{3,2,1,0:T(8,128)S(1)}, u32[]{:S(2)}, u32[]{:S(2)}) %collective-permute-start.6) | collective-permute-done | bytes 262176 | tf_op jit(solution)/shard_map/ppermute | solution.py:19
  68.7 0.6 fusion.9
  69.5 7.4 %collective-permute-start.7 = (f32[2,1,256,128]{3,2,1,0:T(8,128)S(1)}, f32[2,1,256,128]{3,2,1,0:T(8,128)S(1)}, u32[]{:S(2)}, u32[]{:S(2)}) collective-permute-start(f32[2,1,256,128]{3,2,1,0:T(8,128)S(1)} %slice.922), channel_id=1, source_target_pairs={{0,1},{1,2},{2,3},{3,4},{4,5},{5,6},{6,7},{7,8},{8,9},{9,10},{10,1... | collective-permute-start | bytes 786440 | tf_op jit(solution)/shard_map/ppermute | solution.py:19
  78.1 0.7 subtract_bitcast_fusion.4
  78.8 1.2 fusion.11
  80.7 1.3 collective-permute-start.8
  82.6 3.2 %collective-permute-done.8 = f32[2,1,256,128]{3,2,1,0:T(8,128)S(1)} collective-permute-done((f32[2,1,256,128]{3,2,1,0:T(8,128)S(1)}, f32[2,1,256,128]{3,2,1,0:T(8,128)S(1)}, u32[]{:S(2)}, u32[]{:S(2)}) %collective-permute-start.8) | collective-permute-done | bytes 262176 | tf_op jit(solution)/shard_map/ppermute | solution.py:19
  86.2 0.6 fusion.12
  87.0 7.9 %collective-permute-start.9 = (f32[2,1,256,128]{3,2,1,0:T(8,128)S(1)}, f32[2,1,256,128]{3,2,1,0:T(8,128)S(1)}, u32[]{:S(2)}, u32[]{:S(2)}) collective-permute-start(f32[2,1,256,128]{3,2,1,0:T(8,128)S(1)} %slice.946), channel_id=1, source_target_pairs={{0,1},{1,2},{2,3},{3,4},{4,5},{5,6},{6,7},{7,8},{8,9},{9,10},{10,1... | collective-permute-start | bytes 786440 | tf_op jit(solution)/shard_map/ppermute | solution.py:19
  94.9 0.6 convolution_bitcast_fusion.2
  96.1 0.7 subtract_bitcast_fusion.2
  96.8 1.0 fusion.14
  98.5 1.5 collective-permute-start.10
  100.6 3.0 %collective-permute-done.10 = f32[2,1,256,128]{3,2,1,0:T(8,128)S(1)} collective-permute-done((f32[2,1,256,128]{3,2,1,0:T(8,128)S(1)}, f32[2,1,256,128]{3,2,1,0:T(8,128)S(1)}, u32[]{:S(2)}, u32[]{:S(2)}) %collective-permute-start.10) | collective-permute-done | bytes 262176 | tf_op jit(solution)/shard_map/ppermute | solution.py:19
  103.9 0.8 fusion.15
  104.8 8.3 %collective-permute-start.11 = (f32[2,1,256,128]{3,2,1,0:T(8,128)S(1)}, f32[2,1,256,128]{3,2,1,0:T(8,128)S(1)}, u32[]{:S(2)}, u32[]{:S(2)}) collective-permute-start(f32[2,1,256,128]{3,2,1,0:T(8,128)S(1)} %slice.970), channel_id=1, source_target_pairs={{0,1},{1,2},{2,3},{3,4},{4,5},{5,6},{6,7},{7,8},{8,9},{9,10},{10,1... | collective-permute-start | bytes 786440 | tf_op jit(solution)/shard_map/ppermute | solution.py:19
  113.1 0.6 convolution_bitcast_fusion
  114.3 0.7 subtract_bitcast_fusion
  115.0 1.4 fusion.17
  116.4 0.6 convolution_bitcast_fusion.1
  117.0 1.1 multiply_add_fusion
  118.2 7.0 %fusion.32 = f32[4,1,2,8,1,1]{3,1,5,4,2,0:T(1,128)S(1)} fusion(f32[2,4,8,4,4,256]{5,4,3,2,1,0:T(4,128)S(1)} %multiply_add_fusion, f32[4,4,4,256,1,1]{3,2,1,0,4,5:T(4,128)S(1)} %maximum_bitcast_fusion), kind=kOutput, calls=%fused_computation.61 | convolution fusion | flops 3145728 | bytes 1114368 | tf_op jit(solution)/shard_map/rcfmxy,cmxy->rmf/dot_general | solution.py:94
  125.2 25.5 %all-gather = f32[32,4,8]{2,1,0:T(4,128)S(1)} all-gather(f32[2,4,8]{2,1,0:T(4,128)S(1)} %fusion.84), channel_id=2, replica_groups=mesh['member'=2,'gx'=16] {'gx'}, dimensions={0}, use_global_device_ids=true | all-gather | bytes 4352 | tf_op jit(solution)/shard_map/all_gather | solution.py:12
  150.7 0.6 reduce_sum.9
  (148 shorter events, 16.9 us)
Async XLA Ops:
  1.6 3.0 %copy-start.9 = (f32[2]{0:T(128)S(1)}, f32[2]{0:T(128)}, u32[]{:S(2)}) copy-start(f32[2]{0:T(128)} %param.14) | copy-start | bytes 28
  1.6 6.2 %copy-start.10 = (f32[2]{0:T(128)S(1)}, f32[2]{0:T(128)}, u32[]{:S(2)}) copy-start(f32[2]{0:T(128)} %param.15) | copy-start | bytes 28
  1.6 6.7 %copy-start.11 = (f32[2]{0:T(128)S(1)}, f32[2]{0:T(128)}, u32[]{:S(2)}) copy-start(f32[2]{0:T(128)} %param.16) | copy-start | bytes 28
  1.6 7.3 %copy-start.8 = (f32[4]{0:T(128)S(1)}, f32[4]{0:T(128)}, u32[]{:S(2)}) copy-start(f32[4]{0:T(128)} %param.13) | copy-start | bytes 52
  1.7 8.0 %copy-start.12 = (f32[8]{0:T(128)S(1)}, f32[8]{0:T(128)}, u32[]{:S(2)}) copy-start(f32[8]{0:T(128)} %param.17) | copy-start | bytes 100
  1.7 8.2 %copy-start.7 = (f32[4,4,4,256]{3,2,1,0:T(4,128)S(1)}, f32[4,4,4,256]{3,2,1,0:T(4,128)}, u32[]{:S(2)}) copy-start(f32[4,4,4,256]{3,2,1,0:T(4,128)} %param.19) | copy-start | bytes 196612
  1.7 9.7 %copy-start.5 = (s32[4,256,128]{2,1,0:T(8,128)S(1)}, s32[4,256,128]{2,1,0:T(8,128)}, u32[]{:S(2)}) copy-start(s32[4,256,128]{2,1,0:T(8,128)} %param.12) | copy-start | bytes 1572868
  1.7 17.2 %collective-permute-start = (f32[2,1,256,128]{3,2,1,0:T(8,128)S(1)}, f32[2,1,256,128]{3,2,1,0:T(8,128)S(1)}, u32[]{:S(2)}, u32[]{:S(2)}) collective-permute-start(f32[2,1,256,128]{3,2,1,0:T(8,128)S(1)} %slice.656), channel_id=1, source_target_pairs={{1,0},{2,1},{3,2},{4,3},{5,4},{6,5},{7,6},{8,7},{9,8},{10,9},{11,1... | collective-permute-start | bytes 786440 | tf_op jit(solution)/shard_map/ppermute | solution.py:19
  17.4 1.4 copy-start
  18.9 1.4 copy-start.1
  20.6 3.2 %copy-start.6 = (s32[4]{0:T(128)S(1)}, s32[4]{0:T(128)}, u32[]{:S(2)}) copy-start(s32[4]{0:T(128)} %param.18) | copy-start | bytes 52
  20.7 4.2 %collective-permute-start.1 = (f32[2,1,256,128]{3,2,1,0:T(8,128)S(1)}, f32[2,1,256,128]{3,2,1,0:T(8,128)S(1)}, u32[]{:S(2)}, u32[]{:S(2)}) collective-permute-start(f32[2,1,256,128]{3,2,1,0:T(8,128)S(1)} %slice.850), channel_id=1, source_target_pairs={{0,1},{1,2},{2,3},{3,4},{4,5},{5,6},{6,7},{7,8},{8,9},{9,10},{10,1... | collective-permute-start | bytes 786440 | tf_op jit(solution)/shard_map/ppermute | solution.py:19
  26.7 7.7 %collective-permute-start.2 = (f32[2,1,256,128]{3,2,1,0:T(8,128)S(1)}, f32[2,1,256,128]{3,2,1,0:T(8,128)S(1)}, u32[]{:S(2)}, u32[]{:S(2)}) collective-permute-start(f32[2,1,256,128]{3,2,1,0:T(8,128)S(1)} %slice.863), channel_id=1, source_target_pairs={{1,0},{2,1},{3,2},{4,3},{5,4},{6,5},{7,6},{8,7},{9,8},{10,9},{11,1... | collective-permute-start | bytes 786440 | tf_op jit(solution)/shard_map/ppermute | solution.py:19
  35.2 8.6 %collective-permute-start.3 = (f32[2,1,256,128]{3,2,1,0:T(8,128)S(1)}, f32[2,1,256,128]{3,2,1,0:T(8,128)S(1)}, u32[]{:S(2)}, u32[]{:S(2)}) collective-permute-start(f32[2,1,256,128]{3,2,1,0:T(8,128)S(1)} %slice.874), channel_id=1, source_target_pairs={{0,1},{1,2},{2,3},{3,4},{4,5},{5,6},{6,7},{7,8},{8,9},{9,10},{10,1... | collective-permute-start | bytes 786440 | tf_op jit(solution)/shard_map/ppermute | solution.py:19
  46.0 5.1 %collective-permute-start.4 = (f32[2,1,256,128]{3,2,1,0:T(8,128)S(1)}, f32[2,1,256,128]{3,2,1,0:T(8,128)S(1)}, u32[]{:S(2)}, u32[]{:S(2)}) collective-permute-start(f32[2,1,256,128]{3,2,1,0:T(8,128)S(1)} %slice.887), channel_id=1, source_target_pairs={{1,0},{2,1},{3,2},{4,3},{5,4},{6,5},{7,6},{8,7},{9,8},{10,9},{11,1... | collective-permute-start | bytes 786440 | tf_op jit(solution)/shard_map/ppermute | solution.py:19
  52.1 8.6 %collective-permute-start.5 = (f32[2,1,256,128]{3,2,1,0:T(8,128)S(1)}, f32[2,1,256,128]{3,2,1,0:T(8,128)S(1)}, u32[]{:S(2)}, u32[]{:S(2)}) collective-permute-start(f32[2,1,256,128]{3,2,1,0:T(8,128)S(1)} %slice.898), channel_id=1, source_target_pairs={{0,1},{1,2},{2,3},{3,4},{4,5},{5,6},{6,7},{7,8},{8,9},{9,10},{10,1... | collective-permute-start | bytes 786440 | tf_op jit(solution)/shard_map/ppermute | solution.py:19
  63.4 5.1 %collective-permute-start.6 = (f32[2,1,256,128]{3,2,1,0:T(8,128)S(1)}, f32[2,1,256,128]{3,2,1,0:T(8,128)S(1)}, u32[]{:S(2)}, u32[]{:S(2)}) collective-permute-start(f32[2,1,256,128]{3,2,1,0:T(8,128)S(1)} %slice.911), channel_id=1, source_target_pairs={{1,0},{2,1},{3,2},{4,3},{5,4},{6,5},{7,6},{8,7},{9,8},{10,9},{11,1... | collective-permute-start | bytes 786440 | tf_op jit(solution)/shard_map/ppermute | solution.py:19
  69.5 8.6 %collective-permute-start.7 = (f32[2,1,256,128]{3,2,1,0:T(8,128)S(1)}, f32[2,1,256,128]{3,2,1,0:T(8,128)S(1)}, u32[]{:S(2)}, u32[]{:S(2)}) collective-permute-start(f32[2,1,256,128]{3,2,1,0:T(8,128)S(1)} %slice.922), channel_id=1, source_target_pairs={{0,1},{1,2},{2,3},{3,4},{4,5},{5,6},{6,7},{7,8},{8,9},{9,10},{10,1... | collective-permute-start | bytes 786440 | tf_op jit(solution)/shard_map/ppermute | solution.py:19
  80.7 5.1 %collective-permute-start.8 = (f32[2,1,256,128]{3,2,1,0:T(8,128)S(1)}, f32[2,1,256,128]{3,2,1,0:T(8,128)S(1)}, u32[]{:S(2)}, u32[]{:S(2)}) collective-permute-start(f32[2,1,256,128]{3,2,1,0:T(8,128)S(1)} %slice.935), channel_id=1, source_target_pairs={{1,0},{2,1},{3,2},{4,3},{5,4},{6,5},{7,6},{8,7},{9,8},{10,9},{11,1... | collective-permute-start | bytes 786440 | tf_op jit(solution)/shard_map/ppermute | solution.py:19
  87.0 9.1 %collective-permute-start.9 = (f32[2,1,256,128]{3,2,1,0:T(8,128)S(1)}, f32[2,1,256,128]{3,2,1,0:T(8,128)S(1)}, u32[]{:S(2)}, u32[]{:S(2)}) collective-permute-start(f32[2,1,256,128]{3,2,1,0:T(8,128)S(1)} %slice.946), channel_id=1, source_target_pairs={{0,1},{1,2},{2,3},{3,4},{4,5},{5,6},{6,7},{7,8},{8,9},{9,10},{10,1... | collective-permute-start | bytes 786440 | tf_op jit(solution)/shard_map/ppermute | solution.py:19
  98.5 5.1 %collective-permute-start.10 = (f32[2,1,256,128]{3,2,1,0:T(8,128)S(1)}, f32[2,1,256,128]{3,2,1,0:T(8,128)S(1)}, u32[]{:S(2)}, u32[]{:S(2)}) collective-permute-start(f32[2,1,256,128]{3,2,1,0:T(8,128)S(1)} %slice.959), channel_id=1, source_target_pairs={{1,0},{2,1},{3,2},{4,3},{5,4},{6,5},{7,6},{8,7},{9,8},{10,9},{11,1... | collective-permute-start | bytes 786440 | tf_op jit(solution)/shard_map/ppermute | solution.py:19
  104.7 9.6 %copy-start.2 = (f32[3,4,256,128]{3,2,1,0:T(8,128)}, f32[3,4,256,128]{3,2,1,0:T(8,128)S(1)}, u32[]{:S(2)}) copy-start(f32[3,4,256,128]{3,2,1,0:T(8,128)S(1)} %fusion.15) | copy-start | bytes 4718596
  104.8 9.5 %collective-permute-start.11 = (f32[2,1,256,128]{3,2,1,0:T(8,128)S(1)}, f32[2,1,256,128]{3,2,1,0:T(8,128)S(1)}, u32[]{:S(2)}, u32[]{:S(2)}) collective-permute-start(f32[2,1,256,128]{3,2,1,0:T(8,128)S(1)} %slice.970), channel_id=1, source_target_pairs={{0,1},{1,2},{2,3},{3,4},{4,5},{5,6},{6,7},{7,8},{8,9},{9,10},{10,1... | collective-permute-start | bytes 786440 | tf_op jit(solution)/shard_map/ppermute | solution.py:19
  116.4 8.8 %copy-start.3 = (f32[3,4,256,128]{3,2,1,0:T(8,128)}, f32[3,4,256,128]{3,2,1,0:T(8,128)S(1)}, u32[]{:S(2)}) copy-start(f32[3,4,256,128]{3,2,1,0:T(8,128)S(1)} %fusion.17) | copy-start | bytes 4718596
  118.2 33.1 %copy-start.4 = (f32[2,4,8,4,4,256]{5,4,3,2,1,0:T(4,128)}, f32[2,4,8,4,4,256]{5,4,3,2,1,0:T(4,128)S(1)}, u32[]{:S(2)}) copy-start(f32[2,4,8,4,4,256]{5,4,3,2,1,0:T(4,128)S(1)} %multiply_add_fusion) | copy-start | bytes 3145732
